TPU v7x, 128 devices: a whole 4x4x4 slice. The times are simulated.
128 devices in a mesh: row: 32 (over z_lo, x, y), pair: 4 (over z_hi, core).
Axes of the slice: x: 4, y: 4, z: 4 (z_hi: 2, z_lo: 2; z = z_hi * 2 + z_lo), core: 2. Of those that a mesh axis runs over, the one named last changes fastest.
Arguments:
- snapshots: float32 [512, 4, 16384], P('row', 'pair'), may hold values from -6 to 6
- plan: int32 [2, 8], replicated, may hold values from 0 to 7, each once within a row
Outputs:
- rotated: float32 [512, 4, 16384], P(None, 'pair', 'row')
Inputs may be any that keep to these rules, and one draw needn't show every extreme that they name: Each row of plan names every block once.
All inputs are finite; a program needn't handle non-finite values.
Results may differ from a plain program's by a relative error of at most 0.00013.
Values sent between devices are 32-bit elements; how exact they have to be, the bound alone decides.
A program may use at most 128 MiB of HBM per device.

v0:
```python
import jax
import jax.numpy as jnp
from jax import lax
from jax.sharding import PartitionSpec as P


def matmul(left, right):
    return jnp.dot(left, right, precision=lax.Precision.HIGHEST, preferred_element_type=jnp.float32)


def cayley(scaled):
    order_size = scaled.shape[0]
    identity = jnp.eye(order_size, dtype=jnp.float32)
    system = identity + matmul(scaled.T, scaled)
    lifted = identity + scaled
    square = matmul(lifted, lifted)
    lower = lax.linalg.cholesky(system)
    middle = lax.linalg.triangular_solve(lower, square, left_side=True, lower=True)
    return lax.linalg.triangular_solve(lower, middle, left_side=True, lower=True, transpose_a=True)


def locate(current, wanted):
    slot_ids = jnp.arange(current.shape[0], dtype=jnp.int32)
    hits = current[None, :] == wanted[:, None]
    return jnp.sum(jnp.where(hits, slot_ids[None, :], 0), axis=1)


def relocate(work, current, target):
    pair_here = lax.axis_index("pair")
    pair_total = lax.axis_size("pair")
    block_width = work.shape[0] // 2
    row_count = work.shape[1]
    wanted = lax.dynamic_slice_in_dim(target, 2 * pair_here, 2)
    positions = locate(current, wanted)
    everything = lax.all_gather(work, "pair", axis=0, tiled=True).reshape(
        2 * pair_total, block_width, row_count
    )
    upper_block = lax.dynamic_index_in_dim(everything, positions[0], 0, keepdims=False)
    lower_block = lax.dynamic_index_in_dim(everything, positions[1], 0, keepdims=False)
    return jnp.concatenate([upper_block, lower_block], axis=0)


def rotate_whole(work):
    order_size = work.shape[0]
    gram = lax.psum(matmul(work, work.T), "row")
    scales = lax.rsqrt(jnp.diagonal(gram))
    normed = gram * scales[:, None] * scales[None, :]
    column_ids = jnp.arange(order_size, dtype=jnp.int32)
    signs = jnp.sign(column_ids[None, :] - column_ids[:, None]).astype(jnp.float32)
    skew = normed * signs
    factor = 1.0 + jnp.sqrt(jnp.sum(skew * skew))
    turn = cayley(skew / factor)
    return matmul(turn.T, work)


def on_device(snapshots, plan):
    arrived = lax.all_to_all(snapshots, "row", split_axis=2, concat_axis=0, tiled=True)
    work = arrived[:, 0, :]
    block_total = plan.shape[1]
    natural_order = jnp.arange(block_total, dtype=jnp.int32)
    current = natural_order
    for round_index in range(plan.shape[0]):
        target = plan[round_index]
        work = relocate(work, current, target)
        current = target
        work = rotate_whole(work)
    work = relocate(work, current, natural_order)
    return work[:, None, :]


def solution(mesh):
    in_specs = (P("row", "pair", None), P())
    out_specs = P(None, "pair", "row")
    return jax.shard_map(
        on_device, mesh=mesh, in_specs=in_specs, out_specs=out_specs, check_vma=False
    )
```

profile of v0, /device:TPU:1, one launch (start us, length us, event | category | flops | bytes accessed | tf_op | source)
XLA Modules:
  0.0 1240.9 jit_solution(9342640069578683527)
XLA Ops:
  6.5 15.5 %copy.30 = f32[16,1,16384]{0,1,2:T(1,128)} copy(f32[16,1,16384]{2,1,0:T(1,128)} %param.7) | data formatting | bytes 2097152 | tf_op args[0]
  22.6 74.5 %reduce.96 = f32[16384,16]{1,0:T(8,128)} reduce(f32[16384,1,16]{2,1,0:T(1,128)} %bitcast.161, f32[]{:T(128)} %broadcast.231), dimensions={1}, to_apply=%bitcast.125.reduce_sub_computation | reduce | bytes 2097156
  97.0 6.1 reshape.185
  103.1 24.7 %all_to_all.15 = f32[32,1,8192]{2,1,0:T(1,128)S(1)} all-to-all(f32[32,1,8192]{2,1,0:T(1,128)S(1)} %reshape.185), channel_id=1, replica_groups=mesh['row'=32,'pair'=4] {'row'}, dimensions={0} | all-to-all | bytes 2097152 | tf_op jit(solution)/shard_map/all_to_all | solution.py:57
  127.9 3.2 reduce.97
  131.1 17.3 %reshape.186 = f32[16384,1,16]{2,1,0:T(1,128)} reshape(f32[32,8192]{1,0:T(8,128)S(1)} %reduce.97) | data formatting | bytes 2097152
  148.3 5.3 copy.37
  153.6 1.6 copy.32
  160.7 34.6 %all-gather.4.cloned.1.call-done = f32[2048,512]{1,0:T(8,128)} async-done(((f32[512,512]{1,0:T(8,128)}), f32[2048,512]{1,0:T(8,128)}) %all-gather.4.cloned.1.call-update) | async-done | bytes 4194320 | tf_op jit(solution)/shard_map/all_gather | solution.py:35
  197.6 2.8 fusion.23
  201.1 287.3 %all-reduce.4.cloned.1.call-done = f32[512,512]{1,0:T(8,128)} async-done(((f32[512,512]{1,0:T(8,128)}), f32[512,512]{1,0:T(8,128)}) %all-reduce.4.cloned.1.call-update) | async-done | bytes 1048592 | tf_op jit(solution)/shard_map/psum | solution.py:45
  488.4 8.6 gather_fusion
  497.0 2.2 multiply_reduce_fusion.1
  499.9 3.9 fusion.139
  504.4 11.7 custom-call.43
  516.7 9.8 custom-call.44
  527.6 12.7 %custom-call.45 = f32[128,128]{1,0:T(8,128)} custom-call(f32[128,128]{1,0:T(8,128)S(1)} %slice.298), custom_call_target="Cholesky" | custom-call | tf_op jit(solution)/shard_map/cholesky/custom-call.5 | solution.py:17
  541.3 1.4 fusion.101
  542.8 9.8 custom-call.46
  553.2 11.7 custom-call.47
  565.0 9.8 custom-call.48
  575.4 11.9 custom-call.49
  593.8 7.9 while.8
  594.4 1.4 bitcast_dynamic-update-slice_fusion.4
  596.4 1.4 bitcast_dynamic-update-slice_fusion.4
  598.4 1.4 bitcast_dynamic-update-slice_fusion.4
  601.7 39.3 %custom-call.51 = f32[4,128,128]{1,2,0:T(8,128)S(1)} custom-call(f32[4,128,128]{2,1,0:T(8,128)S(1)} %get-tuple-element.37), custom_call_target="InvertDiagBlocksLowerTriangular" | custom-call | tf_op jit(solution)/shard_map/triangular_solve/custom-call.8 | solution.py:19
  641.0 2.3 fusion.4
  649.6 2.9 fusion.6
  657.1 57.0 %all-gather.6.cloned.1.call-done = f32[2048,512]{1,0:T(8,128)} async-done(((f32[512,512]{1,0:T(8,128)}), f32[2048,512]{1,0:T(8,128)}) %all-gather.6.cloned.1.call-update) | async-done | bytes 4194320 | tf_op jit(solution)/shard_map/all_gather | solution.py:35
  716.4 2.8 fusion.22
  719.3 287.8 %all-reduce.6.cloned.1.call-done = f32[512,512]{1,0:T(8,128)} async-done(((f32[512,512]{1,0:T(8,128)}), f32[512,512]{1,0:T(8,128)}) %all-reduce.6.cloned.1.call-update) | async-done | bytes 1048592 | tf_op jit(solution)/shard_map/psum | solution.py:45
  1007.2 8.8 gather_fusion.1
  1016.0 2.2 multiply_reduce_fusion
  1018.9 3.9 fusion.136
  1023.4 11.7 custom-call.52
  1035.7 9.8 custom-call.53
  1046.6 12.5 %custom-call.54 = f32[128,128]{1,0:T(8,128)} custom-call(f32[128,128]{1,0:T(8,128)S(1)} %slice.325), custom_call_target="Cholesky" | custom-call | tf_op jit(solution)/shard_map/cholesky/custom-call.5 | solution.py:17
  1061.0 9.8 custom-call.55
  1071.5 11.7 custom-call.56
  1083.2 9.8 custom-call.57
  1093.6 11.9 custom-call.58
  1110.8 7.9 while.9
  1118.7 39.3 %custom-call.60 = f32[4,128,128]{1,2,0:T(8,128)S(1)} custom-call(f32[4,128,128]{2,1,0:T(8,128)S(1)} %get-tuple-element.39), custom_call_target="InvertDiagBlocksLowerTriangular" | custom-call | tf_op jit(solution)/shard_map/triangular_solve/custom-call.8 | solution.py:19
  1158.1 2.3 fusion.5
  1166.6 2.9 fusion.14
  1174.1 57.0 %all-gather.8.cloned.1.call-done = f32[2048,512]{1,0:T(8,128)} async-done(((f32[512,512]{1,0:T(8,128)}), f32[2048,512]{1,0:T(8,128)}) %all-gather.8.cloned.1.call-update) | async-done | bytes 4194320 | tf_op jit(solution)/shard_map/all_gather | solution.py:35
  1232.5 1.7 broadcast_in_dim.27
  (154 shorter events, 50.7 us)
Async XLA Ops:
  6.5 188.8 %all-gather.4.cloned.1.call-start = ((), (), s32[]{:S(2)}) async-start(), calls=%async_computation.1 | async-start | bytes 5242880 | tf_op jit(solution)/shard_map/all_gather | solution.py:35
  148.3 6.9 copy-start.12
  155.2 333.2 %all-reduce.4.cloned.1.call-start = ((), (), s32[]{:S(2)}) async-start(), calls=%async_computation.2 | async-start | bytes 2097152 | tf_op jit(solution)/shard_map/psum | solution.py:45
  196.6 0.8 copy-start.6
  196.6 1.0 copy-start.8
  200.5 513.6 %all-gather.6.cloned.1.call-start = ((), (), s32[]{:S(2)}) async-start(), calls=%async_computation.3 | async-start | bytes 5242880 | tf_op jit(solution)/shard_map/all_gather | solution.py:35
  516.1 0.6 copy-start.10
  526.5 114.5 %copy-start.1 = (f32[512,512]{1,0:T(8,128)S(1)}, f32[512,512]{1,0:T(8,128)}, u32[]{:S(2)}) copy-start(f32[512,512]{1,0:T(8,128)} %all-reduce.4.cloned.1.call-done) | copy-start | bytes 3145732
  645.0 4.6 copy-start.7
  645.0 4.6 copy-start.9
  652.5 354.7 %all-reduce.6.cloned.1.call-start = ((), (), s32[]{:S(2)}) async-start(), calls=%async_computation.4 | async-start | bytes 2097152 | tf_op jit(solution)/shard_map/psum | solution.py:45
  715.4 0.8 copy-start.2
  715.4 1.0 copy-start.4
  719.3 511.9 %all-gather.8.cloned.1.call-start = ((), (), s32[]{:S(2)}) async-start(), calls=%async_computation.5 | async-start | bytes 5242880 | tf_op jit(solution)/shard_map/all_gather | solution.py:35
  1035.1 0.6 copy-start.11
  1045.5 112.5 %copy-start = (f32[512,512]{1,0:T(8,128)S(1)}, f32[512,512]{1,0:T(8,128)}, u32[]{:S(2)}) copy-start(f32[512,512]{1,0:T(8,128)} %all-reduce.6.cloned.1.call-done) | copy-start | bytes 3145732
  1162.0 4.6 copy-start.3
  1162.0 4.6 copy-start.5
  1164.7 4.9 copy-start.13
Sparse Core Ops, SparseCore 0:
  155.3 39.9 all-gather.3
  200.6 287.7 all-reduce.3
  652.6 61.4 all-gather.5
  719.4 287.7 all-reduce.5
  1169.6 61.4 all-gather.7
where the time goes:
time: 1250 us; the launch traced here: 1240 us
  waiting for transfers between devices  724 us (58%)
  other arithmetic  325 us (26%)
  local copies, waits for them, and re-layouts  94.2 us (8%)
  matrix products  40.3 us (3%)
  between operations  32 us (3%)
  blocking collectives  24.7 us (2%)
    psum x2, waiting for transfers between devices, rotate_whole(): gram = lax.psum(matmul(work, work.T), 'row')  575 us
    another operation x30, other arithmetic, cayley(): lower = lax.linalg.cholesky(system)  163 us
    all_gather x3, waiting for transfers between devices, relocate(): lax.all_gather(work, 'pair', axis=0, tiled=True)  149 us
    another operation x5, other arithmetic, cayley(): lax.linalg.triangular_solve(lower, middle, left_side=True, lower=True, tr...  79.4 us
    unnamed x1, other arithmetic  74.5 us
    unnamed x32, local copies, waits for them, and re-layouts  42.6 us
  transfers between devices with their start and end apart: 5, of which 5 were waited for; matrix products, arithmetic and copies ran while one was open for 0% of the time, Pallas kernels for 0%

commit v1 on v0

--- a/solution.py
+++ b/solution.py
@@ -42,7 +42,9 @@
 
 def rotate_whole(work):
     order_size = work.shape[0]
-    gram = lax.psum(matmul(work, work.T), "row")
+    own = matmul(work, work.T)
+    parts = lax.all_gather(own, "row", axis=0, tiled=False)
+    gram = parts.sum(axis=0)
     scales = lax.rsqrt(jnp.diagonal(gram))
     normed = gram * scales[:, None] * scales[None, :]
     column_ids = jnp.arange(order_size, dtype=jnp.int32)

time: 1250 us -> 1360 us (1.088)
  waiting for transfers between devices: 724 us -> 825 us
  other arithmetic: 325 us -> 343 us
    all_gather x0 -> x2, waiting for transfers between devices: none -> 727 us  [rotate_whole(): parts = lax.all_gather(own, 'row', axis=0, tiled=False)]
    psum x2 -> x0, waiting for transfers between devices: 575 us -> none  [rotate_whole(): gram = lax.psum(matmul(work, work.T), 'row')]
    all_gather x3, waiting for transfers between devices: 149 us -> 98.4 us  [relocate(): lax.all_gather(work, 'pair', axis=0, tiled=True)]
    reduce_sum x0 -> x2, other arithmetic: none -> 24.6 us  [rotate_whole(): gram = parts.sum(axis=0)]
    unnamed x32 -> x22, local copies, waits for them, and re-layouts: 42.6 us -> 41.3 us
where the time goes in v1:
time: 1360 us
  waiting for transfers between devices  825 us (61%)
  other arithmetic  343 us (25%)
  local copies, waits for them, and re-layouts  83.3 us (6%)
  matrix products  46.8 us (3%)
  between operations  31.6 us (2%)
  blocking collectives  24.6 us (2%)
    all_gather x2, waiting for transfers between devices, rotate_whole(): parts = lax.all_gather(own, 'row', axis=0, tiled=False)  727 us
    another operation x30, other arithmetic, cayley(): lower = lax.linalg.cholesky(system)  159 us
    all_gather x3, waiting for transfers between devices, relocate(): lax.all_gather(work, 'pair', axis=0, tiled=True)  98.4 us
    another operation x5, other arithmetic, cayley(): lax.linalg.triangular_solve(lower, middle, left_side=True, lower=True, tr...  79.5 us
    unnamed x1, other arithmetic  74.5 us
    unnamed x22, local copies, waits for them, and re-layouts  41.3 us
  transfers between devices with their start and end apart: 5, of which 5 were waited for; matrix products, arithmetic and copies ran while one was open for 0% of the time, Pallas kernels for 0%

profile of v1, /device:TPU:1, one launch (start us, length us, event | category | flops | bytes accessed | tf_op | source)
XLA Modules:
  0.0 1355.3 jit_solution(11180873061655975761)
XLA Ops:
  6.5 15.5 %copy.30 = f32[16,1,16384]{0,1,2:T(1,128)} copy(f32[16,1,16384]{2,1,0:T(1,128)} %param.7) | data formatting | bytes 2097152 | tf_op args[0]
  22.6 74.5 %reduce.96 = f32[16384,16]{1,0:T(8,128)} reduce(f32[16384,1,16]{2,1,0:T(1,128)} %bitcast.163, f32[]{:T(128)} %broadcast.231), dimensions={1}, to_apply=%bitcast.127.reduce_sub_computation | reduce | bytes 2097156
  97.0 6.1 reshape.187
  103.1 24.6 %all_to_all.15 = f32[32,1,8192]{2,1,0:T(1,128)S(1)} all-to-all(f32[32,1,8192]{2,1,0:T(1,128)S(1)} %reshape.187), channel_id=1, replica_groups=mesh['row'=32,'pair'=4] {'row'}, dimensions={0} | all-to-all | bytes 2097152 | tf_op jit(solution)/shard_map/all_to_all | solution.py:59
  127.7 3.2 reduce.97
  130.9 17.3 %reshape.188 = f32[16384,1,16]{2,1,0:T(1,128)} reshape(f32[32,8192]{1,0:T(8,128)S(1)} %reduce.97) | data formatting | bytes 2097152
  148.2 5.3 copy.37
  153.4 1.6 copy.32
  159.8 35.4 %all-gather.8.cloned.1.call-done = f32[2048,512]{1,0:T(8,128)} async-done(((f32[512,512]{1,0:T(8,128)}), f32[2048,512]{1,0:T(8,128)}) %all-gather.8.cloned.1.call-update) | async-done | bytes 4194320 | tf_op jit(solution)/shard_map/all_gather | solution.py:35
  197.4 2.8 fusion.23
  200.4 363.4 %all-gather.14.cloned.1.call-done = f32[16384,512]{1,0:T(8,128)} async-done(((f32[512,512]{1,0:T(8,128)}), f32[16384,512]{1,0:T(8,128)}) %all-gather.14.cloned.1.call-update) | async-done | bytes 33554448 | tf_op jit(solution)/shard_map/all_gather | solution.py:46
  563.8 12.3 reduce_sum.64
  576.0 5.0 gather_fusion
  582.8 2.4 fusion.139
  585.2 3.2 fusion.4
  589.0 11.7 custom-call.43
  600.9 9.8 custom-call.44
  612.0 11.7 custom-call.45
  625.1 9.8 custom-call.46
  635.5 11.7 custom-call.47
  648.0 10.0 custom-call.48
  658.6 11.7 custom-call.49
  673.7 8.1 while.8
  681.9 39.7 %custom-call.51 = f32[4,128,128]{1,2,0:T(8,128)S(1)} custom-call(f32[4,128,128]{2,1,0:T(8,128)S(1)} %get-tuple-element.37), custom_call_target="InvertDiagBlocksLowerTriangular" | custom-call | tf_op jit(solution)/shard_map/triangular_solve/custom-call.8 | solution.py:19
  721.6 1.4 fusion.61
  724.7 1.4 convolution_subtract_fusion.6
  726.6 1.6 convolution_subtract_fusion.11
  731.7 2.9 fusion.6
  738.9 31.6 %all-gather.10.cloned.1.call-done = f32[2048,512]{1,0:T(8,128)} async-done(((f32[512,512]{1,0:T(8,128)}), f32[2048,512]{1,0:T(8,128)}) %all-gather.10.cloned.1.call-update) | async-done | bytes 4194320 | tf_op jit(solution)/shard_map/all_gather | solution.py:35
  772.8 2.8 fusion.22
  775.7 363.4 %all-gather.16.cloned.1.call-done = f32[16384,512]{1,0:T(8,128)} async-done(((f32[512,512]{1,0:T(8,128)}), f32[16384,512]{1,0:T(8,128)}) %all-gather.16.cloned.1.call-update) | async-done | bytes 33554448 | tf_op jit(solution)/shard_map/all_gather | solution.py:46
  1139.1 12.3 reduce_sum.67
  1151.4 4.7 gather_fusion.1
  1157.8 2.4 fusion.136
  1160.2 3.2 fusion.5
  1164.0 11.7 custom-call.52
  1175.9 9.8 custom-call.53
  1187.0 11.7 custom-call.54
  1200.1 9.8 custom-call.55
  1210.6 11.7 custom-call.56
  1223.0 10.2 custom-call.57
  1233.8 11.7 custom-call.58
  1249.0 8.1 while.9
  1257.1 39.5 %custom-call.60 = f32[4,128,128]{1,2,0:T(8,128)S(1)} custom-call(f32[4,128,128]{2,1,0:T(8,128)S(1)} %get-tuple-element.39), custom_call_target="InvertDiagBlocksLowerTriangular" | custom-call | tf_op jit(solution)/shard_map/triangular_solve/custom-call.8 | solution.py:19
  1301.6 1.6 convolution_subtract_fusion.9
  1306.7 2.9 fusion.14
  1314.2 31.4 %all-gather.12.cloned.1.call-done = f32[2048,512]{1,0:T(8,128)} async-done(((f32[512,512]{1,0:T(8,128)}), f32[2048,512]{1,0:T(8,128)}) %all-gather.12.cloned.1.call-update) | async-done | bytes 4194320 | tf_op jit(solution)/shard_map/all_gather | solution.py:35
  1346.9 1.7 broadcast_in_dim.27
  (146 shorter events, 53.5 us)
Async XLA Ops:
  6.5 188.6 %all-gather.8.cloned.1.call-start = ((), (), s32[]{:S(2)}) async-start(), calls=%async_computation.1 | async-start | bytes 5242880 | tf_op jit(solution)/shard_map/all_gather | solution.py:35
  148.2 6.9 copy-start.8
  155.0 408.7 %all-gather.14.cloned.1.call-start = ((), (), s32[]{:S(2)}) async-start(), calls=%async_computation.4 | async-start | bytes 34603008 | tf_op jit(solution)/shard_map/all_gather | solution.py:46
  196.4 0.8 copy-start.4
  196.4 1.0 copy-start.6
  200.3 570.3 %all-gather.10.cloned.1.call-start = ((), (), s32[]{:S(2)}) async-start(), calls=%async_computation.2 | async-start | bytes 5242880 | tf_op jit(solution)/shard_map/all_gather | solution.py:35
  726.1 5.5 copy-start.5
  726.1 5.5 copy-start.7
  734.6 404.5 %all-gather.16.cloned.1.call-start = ((), (), s32[]{:S(2)}) async-start(), calls=%async_computation.5 | async-start | bytes 34603008 | tf_op jit(solution)/shard_map/all_gather | solution.py:46
  771.8 0.8 copy-start
  771.8 1.0 copy-start.2
  775.6 569.9 %all-gather.12.cloned.1.call-start = ((), (), s32[]{:S(2)}) async-start(), calls=%async_computation.3 | async-start | bytes 5242880 | tf_op jit(solution)/shard_map/all_gather | solution.py:35
  1301.1 5.5 copy-start.1
  1301.1 5.5 copy-start.3
Sparse Core Ops, SparseCore 0:
  155.1 39.9 all-gather.7
  200.4 363.3 all-gather.13
  734.7 35.7 all-gather.9
  775.8 363.3 all-gather.15
  1309.7 35.7 all-gather.11
